TPU v7x, 256 devices: a whole 4x4x8 slice. The times are simulated.
256 devices in a mesh: seq: 64 (over y, z, core), tp: 4 (over x).
Axes of the slice: x: 4, y: 4, z: 8, core: 2. Of those that a mesh axis runs over, the one named last changes fastest.
Arguments:
- normed_input: bfloat16 [32768, 5376], P('seq', 'tp'), may hold values from -6 to 6
- query: bfloat16 [32768, 4096], P('seq', 'tp'), may hold values from -220 to 220, as said below
- key: bfloat16 [32768, 2048], P('seq', 'tp'), may hold values from -7 to 7
- value: bfloat16 [32768, 2048], P('seq', 'tp'), may hold values from -6 to 6
- adapter_down_maps: bfloat16 [64, 16, 5376], P(None, None, 'tp'), may hold values from -0.078125 to 0.078125
- adapter_up_maps: bfloat16 [64, 16, 2048], P(None, None, 'tp'), may hold values from -1.5 to 1.5
- block_adapter_choice: int32 [16], replicated, may hold values from 0 to 63
Outputs:
- attended: bfloat16 [32768, 4096], P('seq', 'tp')
Inputs may be any that keep to these rules, and one draw needn't show every extreme that they name: `query`: queries; some may be aligned with nearby keys.
All inputs are finite; a program needn't handle non-finite values.
Results may differ from a plain program's by a relative error of at most 0.014.
Values may be sent and summed in bfloat16 or wider, within the bound.
A program may use at most 128 MiB of HBM per device.

v0:
```python
import jax
import jax.numpy as jnp
from jax import lax
from jax.sharding import PartitionSpec as P

HEAD_WIDTH = 128
WINDOW = 1024
ADAPTER_RANK = 16
SEG_LEN = 2048
query_scale = 168.0 ** (-0.5)


def shifted(value, axis, steps):
    count = lax.axis_size(axis)
    leading, last = (max(0, -steps), min(count, count - steps))
    return lax.ppermute(value, axis, [(source, source + steps) for source in range(leading, last)])


def on_device(
    normed_input, query, key, value, adapter_down_maps, adapter_up_maps, block_adapter_choice
):
    tok = query.shape[0]
    columns = key.shape[1]
    kv_local = columns // HEAD_WIDTH
    q_local = query.shape[1] // HEAD_WIDTH
    group = q_local // kv_local
    where_seq = lax.axis_index("seq")
    blk = min(tok, SEG_LEN)
    nblk = tok // blk
    last_seg = block_adapter_choice.shape[0] - 1
    token_rows = where_seq * tok + jnp.arange(nblk, dtype=jnp.int32) * blk
    segment_adapter_ids = block_adapter_choice[jnp.clip(token_rows // SEG_LEN, 0, last_seg)]
    selected_down = adapter_down_maps[segment_adapter_ids]
    partial_value = jnp.einsum(
        "bsd,brd->bsr",
        normed_input.reshape(nblk, blk, -1),
        selected_down,
        preferred_element_type=jnp.float32,
    )
    rank_activation = lax.psum(partial_value.reshape(tok, ADAPTER_RANK).astype(jnp.bfloat16), "tp")
    hops = WINDOW // tok
    selected_up = adapter_up_maps[segment_adapter_ids]
    value_update = jnp.einsum(
        "bsr,brc->bsc",
        rank_activation.reshape(nblk, blk, ADAPTER_RANK),
        selected_up,
        preferred_element_type=jnp.float32,
    )
    value_full = (value + value_update.reshape(tok, columns)).astype(jnp.bfloat16)
    pieces = []
    current = (key, value_full)
    for step in range(hops):
        current = shifted((current[0], current[1]), "seq", 1)
        pieces.append((step + 1, current))
    received = pieces[::-1]
    rim_keys = [piece[1][0] for piece in received]
    rim_vals = [piece[1][1] for piece in received]
    keys_all = jnp.concatenate(rim_keys + [key], axis=0)
    vals_all = jnp.concatenate(rim_vals + [value_full], axis=0)
    qblock = min(512, tok)
    span = qblock + WINDOW
    start_global = where_seq * tok

    def one_block(index):
        first = index * qblock
        qrows = query.reshape(qblock, kv_local, group, HEAD_WIDTH)
        krows = keys_all.reshape(span, kv_local, HEAD_WIDTH)
        vrows = vals_all.reshape(span, kv_local, HEAD_WIDTH)
        scores = (
            jnp.einsum("qkgd,lkd->kgql", qrows, krows, preferred_element_type=jnp.float32)
            * query_scale
        )
        qpos = start_global + first + jnp.arange(qblock, dtype=jnp.int32)[:, None]
        kpos = start_global + first - WINDOW + jnp.arange(span, dtype=jnp.int32)[None, :]
        usable = (kpos <= qpos) & (qpos - kpos < WINDOW) & (kpos >= 0)
        scores = jnp.where(usable, scores, -1e30)
        top = jnp.max(scores, axis=-1, keepdims=True)
        expo = jnp.exp(scores - top)
        weights = (expo / jnp.sum(expo, axis=-1, keepdims=True)).astype(jnp.bfloat16)
        out = jnp.einsum("kgql,lkd->qkgd", weights, vrows, preferred_element_type=jnp.float32)
        return out.astype(jnp.bfloat16).reshape(qblock, q_local * HEAD_WIDTH)

    blocks = lax.map(one_block, jnp.arange(tok // qblock, dtype=jnp.int32))
    return blocks.reshape(tok, q_local * HEAD_WIDTH)


def solution(mesh):
    placed = (
        P("seq", "tp"),
        P("seq", "tp"),
        P("seq", "tp"),
        P("seq", "tp"),
        P(None, None, "tp"),
        P(None, None, "tp"),
        P(),
    )
    return jax.shard_map(
        on_device, mesh=mesh, in_specs=placed, out_specs=P("seq", "tp"), check_vma=False
    )
```

profile of v0, /device:TPU:16, one launch (start us, length us, event | category | flops | bytes accessed | tf_op | source)
XLA Modules:
  0.0 97.9 jit_solution(14657647938584223890)
XLA Ops:
  0.0 0.0 copy-start
  0.0 1.4 %dynamic-slice.8 = s32[1]{0:T(128)} dynamic-slice(s32[16]{0:T(128)} %param.13, s32[]{:T(128)} %bitcast.1), dynamic_slice_sizes={1} | dynamic-slice | bytes 12 | tf_op jit(solution)/shard_map/gather | solution.py:32
  3.1 0.0 copy-done
  3.1 1.6 %fusion.12 = bf16[512,16]{0,1:T(8,128)(2,1)S(1)} fusion(bf16[512,1344]{0,1:T(8,128)(2,1)} %param.7, bf16[64,16,1344]{2,1,0:T(8,128)(2,1)S(1)} %copy-done, s32[]{:T(128)} %bitcast.2), kind=kOutput, calls=%fused_computation.19 | convolution fusion | flops 22028288 | bytes 1437700 | tf_op jit(solution)/shard_map/bsd,brd->bsr/dot_general | solution.py:34
  4.7 16.9 %psum.7 = bf16[512,16]{0,1:T(8,128)(2,1)S(1)} all-reduce(bf16[512,16]{0,1:T(8,128)(2,1)S(1)} %fusion.12), channel_id=1, replica_groups=mesh['seq'=64,'tp'=4] {'tp'}, use_global_device_ids=true, to_apply=%region_0.1 | all-reduce | flops 8192 | bytes 32768 | tf_op jit(solution)/shard_map/psum | solution.py:40
  21.6 2.2 %fusion.11 = bf16[512,512]{1,0:T(8,128)(2,1)} fusion(bf16[512,16]{0,1:T(8,128)(2,1)S(1)} %psum.7, bf16[512,512]{1,0:T(8,128)(2,1)} %param.10, bf16[64,16,512]{2,1,0:T(8,128)(2,1)} %param.12, s32[]{:T(128)} %bitcast.2), kind=kOutput, calls=%fused_computation.17 | convolution fusion | flops 9175040 | bytes 1081856 | tf_op jit(solution)/shard_map/bsr,brc->bsc/dot_general | solution.py:43
  23.8 1.9 %collective-permute-start = (bf16[512,512]{1,0:T(8,128)(2,1)}, bf16[512,512]{1,0:T(8,128)(2,1)}, u32[]{:S(2)}, u32[]{:S(2)}) collective-permute-start(bf16[512,512]{1,0:T(8,128)(2,1)} %fusion.11), channel_id=1, source_target_pairs={{0,4},{4,8},{8,12},{12,16},{16,20},{20,24},{24,28},{28,32},{32,36}... | collective-permute-start | bytes 1572872 | tf_op jit(solution)/shard_map/ppermute | solution.py:16
  25.7 1.3 %copy.12 = bf16[512,512]{0,1:T(8,128)(2,1)S(1)} copy(bf16[512,512]{1,0:T(8,128)(2,1)} %param.9) | data formatting | bytes 1048576 | tf_op args[2]
  27.0 3.9 %collective-permute-start.2 = (bf16[512,512]{0,1:T(8,128)(2,1)S(1)}, bf16[512,512]{0,1:T(8,128)(2,1)}, u32[]{:S(2)}, u32[]{:S(2)}) collective-permute-start(bf16[512,512]{0,1:T(8,128)(2,1)S(1)} %copy.12), channel_id=1, source_target_pairs={{0,4},{4,8},{8,12},{12,16},{16,20},{20,24},{24,28},{28,32},{32,36}... | collective-permute-start | bytes 1572872 | tf_op jit(solution)/shard_map/ppermute | solution.py:16
  30.9 5.8 %collective-permute-done = bf16[512,512]{1,0:T(8,128)(2,1)} collective-permute-done((bf16[512,512]{1,0:T(8,128)(2,1)}, bf16[512,512]{1,0:T(8,128)(2,1)}, u32[]{:S(2)}, u32[]{:S(2)}) %collective-permute-start) | collective-permute-done | bytes 524320 | tf_op jit(solution)/shard_map/ppermute | solution.py:16
  36.7 1.9 %collective-permute-start.1 = (bf16[512,512]{1,0:T(8,128)(2,1)}, bf16[512,512]{1,0:T(8,128)(2,1)}, u32[]{:S(2)}, u32[]{:S(2)}) collective-permute-start(bf16[512,512]{1,0:T(8,128)(2,1)} %collective-permute-done), channel_id=1, source_target_pairs={{0,4},{4,8},{8,12},{12,16},{16,20},{20,24},{24,28},{28,32},{32,36}... | collective-permute-start | bytes 1572872 | tf_op jit(solution)/shard_map/ppermute | solution.py:16
  38.6 2.6 %reshape.60 = bf16[512,4,2,128]{3,2,1,0:T(2,128)(2,1)} reshape(bf16[512,1024]{1,0:T(8,128)(2,1)} %param.8) | data formatting | bytes 2097152 | tf_op jit(solution)/shard_map/while/body/eval_jaxpr/reshape | solution.py:66
  41.2 1.1 %collective-permute-done.2 = bf16[512,512]{0,1:T(8,128)(2,1)} collective-permute-done((bf16[512,512]{0,1:T(8,128)(2,1)S(1)}, bf16[512,512]{0,1:T(8,128)(2,1)}, u32[]{:S(2)}, u32[]{:S(2)}) %collective-permute-start.2) | collective-permute-done | bytes 524320 | tf_op jit(solution)/shard_map/ppermute | solution.py:16
  42.3 1.9 %collective-permute-start.3 = (bf16[512,512]{0,1:T(8,128)(2,1)}, bf16[512,512]{0,1:T(8,128)(2,1)}, u32[]{:S(2)}, u32[]{:S(2)}) collective-permute-start(bf16[512,512]{0,1:T(8,128)(2,1)} %collective-permute-done.2), channel_id=1, source_target_pairs={{0,4},{4,8},{8,12},{12,16},{16,20},{20,24},{24,28},{28,32},{32,36}... | collective-permute-start | bytes 1572872 | tf_op jit(solution)/shard_map/ppermute | solution.py:16
  44.3 1.9 %fusion.9 = pred[512,1536]{0,1:T(8,128)(4,1)} fusion(s32[512]{0:T(512)S(1)} %iota_add_fusion.1, s32[1536]{0:T(1024)S(1)} %iota_add_fusion, pred[1536]{0:T(1024)(128)(4,1)S(1)} %broadcast_compare_fusion), kind=kLoop, calls=%fused_computation.12 | loop fusion | flops 3932160 | bytes 796160 | tf_op jit(solution)/shard_map/while/body/eval_jaxpr/and | solution.py:75
  46.2 3.5 %collective-permute-done.1 = bf16[512,512]{1,0:T(8,128)(2,1)} collective-permute-done((bf16[512,512]{1,0:T(8,128)(2,1)}, bf16[512,512]{1,0:T(8,128)(2,1)}, u32[]{:S(2)}, u32[]{:S(2)}) %collective-permute-start.1) | collective-permute-done | bytes 524320 | tf_op jit(solution)/shard_map/ppermute | solution.py:16
  49.6 2.6 %pad_maximum_fusion = bf16[1536,512]{1,0:T(8,128)(2,1)} fusion(bf16[512,512]{1,0:T(8,128)(2,1)} %fusion.11, bf16[512,512]{1,0:T(8,128)(2,1)} %collective-permute-done, bf16[512,512]{1,0:T(8,128)(2,1)} %collective-permute-done.1), kind=kLoop, calls=%fused_computation.13 | loop fusion | flops 4718592 | bytes 3145728 | tf_op jit(solution)/shard_map/concatenate | solution.py:59
  52.2 2.6 %copy.22 = bf16[1536,512]{0,1:T(8,128)(2,1)} copy(bf16[1536,512]{1,0:T(8,128)(2,1)} %pad_maximum_fusion) | data formatting | bytes 3145728 | tf_op jit(solution)/shard_map/while/body/eval_jaxpr/reshape | solution.py:68
  54.9 0.0 copy-start.2
  54.9 0.4 collective-permute-done.3
  55.3 1.3 %pad_maximum_fusion.1 = bf16[1536,512]{0,1:T(8,128)(2,1)S(1)} fusion(bf16[512,512]{0,1:T(8,128)(2,1)S(1)} %copy.12, bf16[512,512]{0,1:T(8,128)(2,1)} %collective-permute-done.2, bf16[512,512]{0,1:T(8,128)(2,1)} %collective-permute-done.3), kind=kLoop, calls=%fused_computation.14 | loop fusion | flops 4718592 | bytes 3145728 | tf_op jit(solution)/shard_map/concatenate | solution.py:58
  56.6 0.0 copy-start.1
  56.6 1.1 %copy-done.1 = bf16[1536,512]{0,1:T(8,128)(2,1)} copy-done((bf16[1536,512]{0,1:T(8,128)(2,1)}, bf16[1536,512]{0,1:T(8,128)(2,1)S(1)}, u32[]{:S(2)}) %copy-start.1) | copy-done | bytes 1572888
  57.7 0.0 copy-done.2
  57.7 11.8 %fusion.15 = f32[4,1536,512,2]{2,1,3,0:T(8,128)} fusion(bf16[1536,4,128,1]{0,2,3,1:T(8,128)(2,1)S(1)} %bitcast.42, bf16[512,4,2,128]{3,2,1,0:T(2,128)(2,1)S(1)} %copy-done.2), kind=kOutput, calls=%fused_computation.21 | convolution fusion | flops 1610612736 | bytes 27787264 | tf_op jit(solution)/shard_map/while/body/eval_jaxpr/qkgd,lkd->kgql/dot_general | solution.py:70
  69.5 10.9 %fusion.30 = f32[4,2,512]{2,1,0:T(2,128)S(1)} fusion(pred[512,1536]{0,1:T(8,128)(4,1)} %fusion.9, bf16[1536,4,128,1]{0,2,3,1:T(8,128)(2,1)} %bitcast.43, bf16[512,4,2,128]{3,2,1,0:T(2,128)(2,1)} %reshape.60), kind=kOutput, calls=%fused_computation.37 | convolution fusion | flops 1635780096 | bytes 3424256 | tf_op jit(solution)/shard_map/while/body/eval_jaxpr/sub | solution.py:78
  80.4 15.2 %fusion.10 = bf16[4,128,2,512]{3,1,2,0:T(8,128)(2,1)} fusion(bf16[1536,4,128,1]{0,2,3,1:T(8,128)(2,1)} %bitcast.44, f32[4,2,512]{2,1,0:T(2,128)S(1)} %fusion.30, f32[4,1536,512,2]{2,1,3,0:T(8,128)} %fusion.15, pred[512,1536]{0,1:T(8,128)(4,1)} %fusion.9), kind=kOutput, calls=%fused_computation.15 | convolution fusion | flops 1642599936 | bytes 28590080 | tf_op jit(solution)/shard_map/while/body/eval_jaxpr/kgql,lkd->qkgd/dot_general | solution.py:80
  95.6 2.3 %copy.18 = bf16[512,1024]{1,0:T(8,128)(2,1)} copy(bf16[512,1024]{0,1:T(8,128)(2,1)} %bitcast.45) | data formatting | bytes 2097152 | tf_op jit(solution)/shard_map/reshape | solution.py:84
  (3 shorter events, 0.0 us)
Async XLA Ops:
  0.0 3.1 %copy-start = (bf16[64,16,1344]{2,1,0:T(8,128)(2,1)S(1)}, bf16[64,16,1344]{2,1,0:T(8,128)(2,1)}, u32[]{:S(2)}) copy-start(bf16[64,16,1344]{2,1,0:T(8,128)(2,1)} %param.11) | copy-start | bytes 8257540
  23.8 12.9 %collective-permute-start = (bf16[512,512]{1,0:T(8,128)(2,1)}, bf16[512,512]{1,0:T(8,128)(2,1)}, u32[]{:S(2)}, u32[]{:S(2)}) collective-permute-start(bf16[512,512]{1,0:T(8,128)(2,1)} %fusion.11), channel_id=1, source_target_pairs={{0,4},{4,8},{8,12},{12,16},{16,20},{20,24},{24,28},{28,32},{32,36}... | collective-permute-start | bytes 1572872 | tf_op jit(solution)/shard_map/ppermute | solution.py:16
  27.0 15.4 %collective-permute-start.2 = (bf16[512,512]{0,1:T(8,128)(2,1)S(1)}, bf16[512,512]{0,1:T(8,128)(2,1)}, u32[]{:S(2)}, u32[]{:S(2)}) collective-permute-start(bf16[512,512]{0,1:T(8,128)(2,1)S(1)} %copy.12), channel_id=1, source_target_pairs={{0,4},{4,8},{8,12},{12,16},{16,20},{20,24},{24,28},{28,32},{32,36}... | collective-permute-start | bytes 1572872 | tf_op jit(solution)/shard_map/ppermute | solution.py:16
  36.7 12.9 %collective-permute-start.1 = (bf16[512,512]{1,0:T(8,128)(2,1)}, bf16[512,512]{1,0:T(8,128)(2,1)}, u32[]{:S(2)}, u32[]{:S(2)}) collective-permute-start(bf16[512,512]{1,0:T(8,128)(2,1)} %collective-permute-done), channel_id=1, source_target_pairs={{0,4},{4,8},{8,12},{12,16},{16,20},{20,24},{24,28},{28,32},{32,36}... | collective-permute-start | bytes 1572872 | tf_op jit(solution)/shard_map/ppermute | solution.py:16
  42.3 12.9 %collective-permute-start.3 = (bf16[512,512]{0,1:T(8,128)(2,1)}, bf16[512,512]{0,1:T(8,128)(2,1)}, u32[]{:S(2)}, u32[]{:S(2)}) collective-permute-start(bf16[512,512]{0,1:T(8,128)(2,1)} %collective-permute-done.2), channel_id=1, source_target_pairs={{0,4},{4,8},{8,12},{12,16},{16,20},{20,24},{24,28},{28,32},{32,36}... | collective-permute-start | bytes 1572872 | tf_op jit(solution)/shard_map/ppermute | solution.py:16
  54.9 2.8 %copy-start.2 = (bf16[512,4,2,128]{3,2,1,0:T(2,128)(2,1)S(1)}, bf16[512,4,2,128]{3,2,1,0:T(2,128)(2,1)}, u32[]{:S(2)}) copy-start(bf16[512,4,2,128]{3,2,1,0:T(2,128)(2,1)} %reshape.60) | copy-start | bytes 3145732
  56.6 1.1 %copy-start.1 = (bf16[1536,512]{0,1:T(8,128)(2,1)}, bf16[1536,512]{0,1:T(8,128)(2,1)S(1)}, u32[]{:S(2)}) copy-start(bf16[1536,512]{0,1:T(8,128)(2,1)S(1)} %pad_maximum_fusion.1) | copy-start | bytes 4718596
where the time goes:
time: 98.3 us; the launch traced here: 97.9 us
  matrix products  41.7 us (42%)
  blocking collectives  16.9 us (17%)
  local copies, waits for them, and re-layouts  11.3 us (11%)
  waiting for transfers between devices  10.7 us (11%)
  starting transfers between devices  9.66 us (10%)
  other arithmetic  5.86 us (6%)
  between operations  1.78 us (2%)
    psum x1, blocking collectives, on_device(): lax.psum(partial_value.reshape(tok, ADAPTER_RANK).astype(jnp.bfloat16), '...  16.9 us
    dot_general x1, matrix products, one_block(): jnp.einsum('kgql,lkd->qkgd', weights, vrows, preferred_element_type=jnp.f...  15.2 us
    dot_general x1, matrix products, one_block(): jnp.einsum('qkgd,lkd->kgql', qrows, krows, preferred_element_type=jnp.flo...  11.8 us
    sub x1, matrix products, one_block(): expo = jnp.exp(scores - top)  10.9 us
    ppermute x4, waiting for transfers between devices, shifted(): lax.ppermute(value, axis, [(source, source + steps) for source in range(l...  10.7 us
    ppermute x4, starting transfers between devices, shifted(): lax.ppermute(value, axis, [(source, source + steps) for source in range(l...  9.66 us
    reshape x1, local copies, waits for them, and re-layouts, one_block(): vrows = vals_all.reshape(span, kv_local, HEAD_WIDTH)  2.64 us
    concatenate x1, other arithmetic, on_device(): vals_all = jnp.concatenate(rim_vals + [value_full], axis=0)  2.61 us
  transfers between devices with their start and end apart: 4, of which 4 were waited for; matrix products, arithmetic and copies ran while one was open for 11% of the time, Pallas kernels for 0%

commit v1 on v0

--- a/solution.py
+++ b/solution.py
@@ -37,7 +37,9 @@
         selected_down,
         preferred_element_type=jnp.float32,
     )
-    rank_activation = lax.psum(partial_value.reshape(tok, ADAPTER_RANK).astype(jnp.bfloat16), "tp")
+    rank_activation = jnp.sum(
+        lax.all_gather(partial_value.reshape(tok, ADAPTER_RANK).astype(jnp.bfloat16), "tp"), axis=0
+    )
     hops = WINDOW // tok
     selected_up = adapter_up_maps[segment_adapter_ids]
     value_update = jnp.einsum(

time: 98.3 us -> 93.8 us (0.954)
  blocking collectives: 16.9 us -> 12.2 us
    psum x1 -> x0, blocking collectives: 16.9 us -> none  [on_device(): lax.psum(partial_value.reshape(tok, ADAPTER_RANK).astype(jnp.bfloat16), '...]
    all_gather x0 -> x1, blocking collectives: none -> 12.2 us  [on_device(): lax.all_gather(partial_value.reshape(tok, ADAPTER_RANK).astype(jnp.bfloat...]
  transfers between devices with their start and end apart: 4 -> 4, of which waited for: 4 -> 4; matrix products, arithmetic and copies ran while one was open for 11% -> 12% of each run, Pallas kernels for 0% -> 0%
where the time goes in v1:
time: 93.8 us; the launch traced here: 93.3 us
  matrix products  41.7 us (44%)
  blocking collectives  12.2 us (13%)
  local copies, waits for them, and re-layouts  11.3 us (12%)
  waiting for transfers between devices  10.7 us (11%)
  starting transfers between devices  9.65 us (10%)
  other arithmetic  5.95 us (6%)
  between operations  1.79 us (2%)
    dot_general x1, matrix products, one_block(): jnp.einsum('kgql,lkd->qkgd', weights, vrows, preferred_element_type=jnp.f...  15.2 us
    all_gather x1, blocking collectives, on_device(): lax.all_gather(partial_value.reshape(tok, ADAPTER_RANK).astype(jnp.bfloat...  12.2 us
    dot_general x1, matrix products, one_block(): jnp.einsum('qkgd,lkd->kgql', qrows, krows, preferred_element_type=jnp.flo...  11.8 us
    sub x1, matrix products, one_block(): expo = jnp.exp(scores - top)  10.9 us
    ppermute x4, waiting for transfers between devices, shifted(): lax.ppermute(value, axis, [(source, source + steps) for source in range(l...  10.7 us
    ppermute x4, starting transfers between devices, shifted(): lax.ppermute(value, axis, [(source, source + steps) for source in range(l...  9.65 us
    reshape x1, local copies, waits for them, and re-layouts, one_block(): vrows = vals_all.reshape(span, kv_local, HEAD_WIDTH)  2.64 us
    concatenate x1, other arithmetic, on_device(): vals_all = jnp.concatenate(rim_vals + [value_full], axis=0)  2.61 us
  transfers between devices with their start and end apart: 4, of which 4 were waited for; matrix products, arithmetic and copies ran while one was open for 12% of the time, Pallas kernels for 0%

profile of v1, /device:TPU:16, one launch (start us, length us, event | category | flops | bytes accessed | tf_op | source)
XLA Modules:
  0.0 93.3 jit_solution(9298967693171076130)
XLA Ops:
  0.0 0.0 copy-start
  0.0 1.4 %dynamic-slice.8 = s32[1]{0:T(128)} dynamic-slice(s32[16]{0:T(128)} %param.13, s32[]{:T(128)} %bitcast.1), dynamic_slice_sizes={1} | dynamic-slice | bytes 12 | tf_op jit(solution)/shard_map/gather | solution.py:32
  3.1 0.0 copy-done
  3.1 1.6 %fusion.12 = bf16[512,16]{0,1:T(8,128)(2,1)S(1)} fusion(bf16[512,1344]{0,1:T(8,128)(2,1)} %param.7, bf16[64,16,1344]{2,1,0:T(8,128)(2,1)S(1)} %copy-done, s32[]{:T(128)} %bitcast.2), kind=kOutput, calls=%fused_computation.19 | convolution fusion | flops 22028288 | bytes 1437700 | tf_op jit(solution)/shard_map/bsd,brd->bsr/dot_general | solution.py:34
  4.7 12.2 %all-gather = bf16[2048,16]{0,1:T(8,128)(2,1)S(1)} all-gather(bf16[512,16]{0,1:T(8,128)(2,1)S(1)} %fusion.12), channel_id=2, replica_groups=mesh['seq'=64,'tp'=4] {'tp'}, dimensions={0}, use_global_device_ids=true | all-gather | bytes 81920 | tf_op jit(solution)/shard_map/all_gather | solution.py:41
  17.0 0.1 reduce_sum.22
  17.0 2.2 %fusion.11 = bf16[512,512]{1,0:T(8,128)(2,1)} fusion(bf16[512,16]{0,1:T(8,128)(2,1)S(1)} %reduce_sum.22, bf16[512,512]{1,0:T(8,128)(2,1)} %param.10, bf16[64,16,512]{2,1,0:T(8,128)(2,1)} %param.12, s32[]{:T(128)} %bitcast.2), kind=kOutput, calls=%fused_computation.17 | convolution fusion | flops 9175040 | bytes 1081856 | tf_op jit(solution)/shard_map/bsr,brc->bsc/dot_general | solution.py:45
  19.2 1.9 %collective-permute-start = (bf16[512,512]{1,0:T(8,128)(2,1)}, bf16[512,512]{1,0:T(8,128)(2,1)}, u32[]{:S(2)}, u32[]{:S(2)}) collective-permute-start(bf16[512,512]{1,0:T(8,128)(2,1)} %fusion.11), channel_id=1, source_target_pairs={{0,4},{4,8},{8,12},{12,16},{16,20},{20,24},{24,28},{28,32},{32,36}... | collective-permute-start | bytes 1572872 | tf_op jit(solution)/shard_map/ppermute | solution.py:16
  21.2 1.3 %copy.19 = bf16[512,512]{0,1:T(8,128)(2,1)S(1)} copy(bf16[512,512]{1,0:T(8,128)(2,1)} %param.9) | data formatting | bytes 1048576 | tf_op args[2]
  22.4 3.9 %collective-permute-start.2 = (bf16[512,512]{0,1:T(8,128)(2,1)S(1)}, bf16[512,512]{0,1:T(8,128)(2,1)}, u32[]{:S(2)}, u32[]{:S(2)}) collective-permute-start(bf16[512,512]{0,1:T(8,128)(2,1)S(1)} %copy.19), channel_id=1, source_target_pairs={{0,4},{4,8},{8,12},{12,16},{16,20},{20,24},{24,28},{28,32},{32,36}... | collective-permute-start | bytes 1572872 | tf_op jit(solution)/shard_map/ppermute | solution.py:16
  26.4 5.8 %collective-permute-done = bf16[512,512]{1,0:T(8,128)(2,1)} collective-permute-done((bf16[512,512]{1,0:T(8,128)(2,1)}, bf16[512,512]{1,0:T(8,128)(2,1)}, u32[]{:S(2)}, u32[]{:S(2)}) %collective-permute-start) | collective-permute-done | bytes 524320 | tf_op jit(solution)/shard_map/ppermute | solution.py:16
  32.2 1.9 %collective-permute-start.1 = (bf16[512,512]{1,0:T(8,128)(2,1)}, bf16[512,512]{1,0:T(8,128)(2,1)}, u32[]{:S(2)}, u32[]{:S(2)}) collective-permute-start(bf16[512,512]{1,0:T(8,128)(2,1)} %collective-permute-done), channel_id=1, source_target_pairs={{0,4},{4,8},{8,12},{12,16},{16,20},{20,24},{24,28},{28,32},{32,36}... | collective-permute-start | bytes 1572872 | tf_op jit(solution)/shard_map/ppermute | solution.py:16
  34.1 2.6 %reshape.62 = bf16[512,4,2,128]{3,2,1,0:T(2,128)(2,1)} reshape(bf16[512,1024]{1,0:T(8,128)(2,1)} %param.8) | data formatting | bytes 2097152 | tf_op jit(solution)/shard_map/while/body/eval_jaxpr/reshape | solution.py:68
  36.7 1.1 %collective-permute-done.2 = bf16[512,512]{0,1:T(8,128)(2,1)} collective-permute-done((bf16[512,512]{0,1:T(8,128)(2,1)S(1)}, bf16[512,512]{0,1:T(8,128)(2,1)}, u32[]{:S(2)}, u32[]{:S(2)}) %collective-permute-start.2) | collective-permute-done | bytes 524320 | tf_op jit(solution)/shard_map/ppermute | solution.py:16
  37.8 1.9 %collective-permute-start.3 = (bf16[512,512]{0,1:T(8,128)(2,1)}, bf16[512,512]{0,1:T(8,128)(2,1)}, u32[]{:S(2)}, u32[]{:S(2)}) collective-permute-start(bf16[512,512]{0,1:T(8,128)(2,1)} %collective-permute-done.2), channel_id=1, source_target_pairs={{0,4},{4,8},{8,12},{12,16},{16,20},{20,24},{24,28},{28,32},{32,36}... | collective-permute-start | bytes 1572872 | tf_op jit(solution)/shard_map/ppermute | solution.py:16
  39.7 1.9 %fusion.9 = pred[512,1536]{0,1:T(8,128)(4,1)} fusion(s32[512]{0:T(512)S(1)} %iota_add_fusion.1, s32[1536]{0:T(1024)S(1)} %iota_add_fusion, pred[1536]{0:T(1024)(128)(4,1)S(1)} %broadcast_compare_fusion), kind=kLoop, calls=%fused_computation.12 | loop fusion | flops 3932160 | bytes 796160 | tf_op jit(solution)/shard_map/while/body/eval_jaxpr/and | solution.py:77
  41.6 3.5 %collective-permute-done.1 = bf16[512,512]{1,0:T(8,128)(2,1)} collective-permute-done((bf16[512,512]{1,0:T(8,128)(2,1)}, bf16[512,512]{1,0:T(8,128)(2,1)}, u32[]{:S(2)}, u32[]{:S(2)}) %collective-permute-start.1) | collective-permute-done | bytes 524320 | tf_op jit(solution)/shard_map/ppermute | solution.py:16
  45.1 2.6 %pad_maximum_fusion = bf16[1536,512]{1,0:T(8,128)(2,1)} fusion(bf16[512,512]{1,0:T(8,128)(2,1)} %fusion.11, bf16[512,512]{1,0:T(8,128)(2,1)} %collective-permute-done, bf16[512,512]{1,0:T(8,128)(2,1)} %collective-permute-done.1), kind=kLoop, calls=%fused_computation.13 | loop fusion | flops 4718592 | bytes 3145728 | tf_op jit(solution)/shard_map/concatenate | solution.py:61
  47.7 2.6 %copy.29 = bf16[1536,512]{0,1:T(8,128)(2,1)} copy(bf16[1536,512]{1,0:T(8,128)(2,1)} %pad_maximum_fusion) | data formatting | bytes 3145728 | tf_op jit(solution)/shard_map/while/body/eval_jaxpr/reshape | solution.py:70
  50.3 0.0 copy-start.2
  50.3 0.4 collective-permute-done.3
  50.7 1.3 %pad_maximum_fusion.1 = bf16[1536,512]{0,1:T(8,128)(2,1)S(1)} fusion(bf16[512,512]{0,1:T(8,128)(2,1)S(1)} %copy.19, bf16[512,512]{0,1:T(8,128)(2,1)} %collective-permute-done.2, bf16[512,512]{0,1:T(8,128)(2,1)} %collective-permute-done.3), kind=kLoop, calls=%fused_computation.14 | loop fusion | flops 4718592 | bytes 3145728 | tf_op jit(solution)/shard_map/concatenate | solution.py:60
  52.0 0.0 copy-start.1
  52.0 1.1 %copy-done.1 = bf16[1536,512]{0,1:T(8,128)(2,1)} copy-done((bf16[1536,512]{0,1:T(8,128)(2,1)}, bf16[1536,512]{0,1:T(8,128)(2,1)S(1)}, u32[]{:S(2)}) %copy-start.1) | copy-done | bytes 1572888
  53.2 0.0 copy-done.2
  53.2 11.8 %fusion.15 = f32[4,1536,512,2]{2,1,3,0:T(8,128)} fusion(bf16[1536,4,128,1]{0,2,3,1:T(8,128)(2,1)S(1)} %bitcast.44, bf16[512,4,2,128]{3,2,1,0:T(2,128)(2,1)S(1)} %copy-done.2), kind=kOutput, calls=%fused_computation.21 | convolution fusion | flops 1610612736 | bytes 27787264 | tf_op jit(solution)/shard_map/while/body/eval_jaxpr/qkgd,lkd->kgql/dot_general | solution.py:72
  64.9 10.9 %fusion.30 = f32[4,2,512]{2,1,0:T(2,128)S(1)} fusion(pred[512,1536]{0,1:T(8,128)(4,1)} %fusion.9, bf16[1536,4,128,1]{0,2,3,1:T(8,128)(2,1)} %bitcast.45, bf16[512,4,2,128]{3,2,1,0:T(2,128)(2,1)} %reshape.62), kind=kOutput, calls=%fused_computation.37 | convolution fusion | flops 1635780096 | bytes 3424256 | tf_op jit(solution)/shard_map/while/body/eval_jaxpr/sub | solution.py:80
  75.8 15.2 %fusion.10 = bf16[4,128,2,512]{3,1,2,0:T(8,128)(2,1)} fusion(bf16[1536,4,128,1]{0,2,3,1:T(8,128)(2,1)} %bitcast.46, f32[4,2,512]{2,1,0:T(2,128)S(1)} %fusion.30, f32[4,1536,512,2]{2,1,3,0:T(8,128)} %fusion.15, pred[512,1536]{0,1:T(8,128)(4,1)} %fusion.9), kind=kOutput, calls=%fused_computation.15 | convolution fusion | flops 1642599936 | bytes 28590080 | tf_op jit(solution)/shard_map/while/body/eval_jaxpr/kgql,lkd->qkgd/dot_general | solution.py:82
  91.0 2.3 %copy.25 = bf16[512,1024]{1,0:T(8,128)(2,1)} copy(bf16[512,1024]{0,1:T(8,128)(2,1)} %bitcast.47) | data formatting | bytes 2097152 | tf_op jit(solution)/shard_map/reshape | solution.py:86
  (4 shorter events, 0.1 us)
Async XLA Ops:
  0.0 3.1 %copy-start = (bf16[64,16,1344]{2,1,0:T(8,128)(2,1)S(1)}, bf16[64,16,1344]{2,1,0:T(8,128)(2,1)}, u32[]{:S(2)}) copy-start(bf16[64,16,1344]{2,1,0:T(8,128)(2,1)} %param.11) | copy-start | bytes 8257540
  19.2 12.9 %collective-permute-start = (bf16[512,512]{1,0:T(8,128)(2,1)}, bf16[512,512]{1,0:T(8,128)(2,1)}, u32[]{:S(2)}, u32[]{:S(2)}) collective-permute-start(bf16[512,512]{1,0:T(8,128)(2,1)} %fusion.11), channel_id=1, source_target_pairs={{0,4},{4,8},{8,12},{12,16},{16,20},{20,24},{24,28},{28,32},{32,36}... | collective-permute-start | bytes 1572872 | tf_op jit(solution)/shard_map/ppermute | solution.py:16
  22.4 15.4 %collective-permute-start.2 = (bf16[512,512]{0,1:T(8,128)(2,1)S(1)}, bf16[512,512]{0,1:T(8,128)(2,1)}, u32[]{:S(2)}, u32[]{:S(2)}) collective-permute-start(bf16[512,512]{0,1:T(8,128)(2,1)S(1)} %copy.19), channel_id=1, source_target_pairs={{0,4},{4,8},{8,12},{12,16},{16,20},{20,24},{24,28},{28,32},{32,36}... | collective-permute-start | bytes 1572872 | tf_op jit(solution)/shard_map/ppermute | solution.py:16
  32.2 12.9 %collective-permute-start.1 = (bf16[512,512]{1,0:T(8,128)(2,1)}, bf16[512,512]{1,0:T(8,128)(2,1)}, u32[]{:S(2)}, u32[]{:S(2)}) collective-permute-start(bf16[512,512]{1,0:T(8,128)(2,1)} %collective-permute-done), channel_id=1, source_target_pairs={{0,4},{4,8},{8,12},{12,16},{16,20},{20,24},{24,28},{28,32},{32,36}... | collective-permute-start | bytes 1572872 | tf_op jit(solution)/shard_map/ppermute | solution.py:16
  37.8 12.9 %collective-permute-start.3 = (bf16[512,512]{0,1:T(8,128)(2,1)}, bf16[512,512]{0,1:T(8,128)(2,1)}, u32[]{:S(2)}, u32[]{:S(2)}) collective-permute-start(bf16[512,512]{0,1:T(8,128)(2,1)} %collective-permute-done.2), channel_id=1, source_target_pairs={{0,4},{4,8},{8,12},{12,16},{16,20},{20,24},{24,28},{28,32},{32,36}... | collective-permute-start | bytes 1572872 | tf_op jit(solution)/shard_map/ppermute | solution.py:16
  50.3 2.8 %copy-start.2 = (bf16[512,4,2,128]{3,2,1,0:T(2,128)(2,1)S(1)}, bf16[512,4,2,128]{3,2,1,0:T(2,128)(2,1)}, u32[]{:S(2)}) copy-start(bf16[512,4,2,128]{3,2,1,0:T(2,128)(2,1)} %reshape.62) | copy-start | bytes 3145732
  52.0 1.1 %copy-start.1 = (bf16[1536,512]{0,1:T(8,128)(2,1)}, bf16[1536,512]{0,1:T(8,128)(2,1)S(1)}, u32[]{:S(2)}) copy-start(bf16[1536,512]{0,1:T(8,128)(2,1)S(1)} %pad_maximum_fusion.1) | copy-start | bytes 4718596
